TPU v7x, 128 devices: a whole 4x4x4 slice. The times are simulated.
128 devices in a mesh: tok: 8 (over x, z_hi), feat: 16 (over y, z_lo, core).
Axes of the slice: x: 4, y: 4, z: 4 (z_hi: 2, z_lo: 2; z = z_hi * 2 + z_lo), core: 2. Of those that a mesh axis runs over, the one named last changes fastest.
Arguments:
- resid: bfloat16 [2048, 8192], P(None, ('tok', 'feat')), may hold values from -6 to 6
- resid_grad: bfloat16 [2048, 8192], P(None, ('tok', 'feat')), may hold values from -6 to 6
- active: int32 [16, 20], P('tok'), may hold values from 0 to 79, all different within a row
- w_enc: bfloat16 [8192, 10240], P(None, 'feat'), may hold values from -0.0625 to 0.0625
- b_enc: float32 [10240], P('feat'), may hold values from -3 to 3
- w_dec: bfloat16 [10240, 8192], P('feat'), may hold values from -0.25 to 0.25
- b_dec: float32 [8192], P('feat'), may hold values from -3 to 3
Outputs:
- feature_attr: float32 [2048, 10240], P('tok', 'feat')
- error: float32 [2048, 8192], P('tok', 'feat')
- error_attr: float32 [2048], P('tok')
Inputs may be any that keep to these rules, and one draw needn't show every extreme that they name: `active`: each row lists 20 different feature blocks; every block is listed by some tile.
All inputs are finite; a program needn't handle non-finite values.
Results may differ from a plain program's by a relative error of at most 0.012.
Values may be sent and summed in bfloat16 or wider, within the bound.
A program may use at most 128 MiB of HBM per device.

v0:
```python
import jax
import jax.numpy as jnp
from jax import lax
from jax.sharding import PartitionSpec as P

BLOCK = 128
TILE = 128


def per_device(resid, resid_grad, active, w_enc, b_enc, w_dec, b_dec):
    n_feat = lax.axis_size("feat")
    width = resid.shape[1]
    cols_x, cols_g = (
        lax.all_gather(resid[:, None, :], "feat", axis=1, tiled=True),
        lax.all_gather(resid_grad[:, None, :], "feat", axis=1, tiled=True),
    )
    total = cols_x.shape[0]
    cols_x = cols_x.reshape(total, n_feat * width)
    cols_g = cols_g.reshape(total, n_feat * width)
    rows_x, rows_g = (
        lax.all_to_all(cols_x, "tok", split_axis=0, concat_axis=1, tiled=True),
        lax.all_to_all(cols_g, "tok", split_axis=0, concat_axis=1, tiled=True),
    )
    tok_rows = rows_x.shape[0]
    feat_dev = w_enc.shape[1]
    blocks = feat_dev // BLOCK
    tiles_dev = active.shape[0]
    block_ids = lax.axis_index("feat") * blocks + jnp.arange(blocks, dtype=jnp.int32)
    hits = jnp.any(active[:, :, None] == block_ids[None, None, :], axis=1).astype(jnp.float32)
    pre = jnp.dot(rows_x, w_enc, preferred_element_type=jnp.float32) + b_enc
    shaped = jnp.maximum(pre, 0.0).reshape(tiles_dev, TILE, blocks, BLOCK) * hits[:, None, :, None]
    acts = shaped.reshape(tok_rows, feat_dev).astype(jnp.bfloat16)
    partial_recon = jnp.dot(acts, w_dec, preferred_element_type=jnp.float32)
    recon_share = lax.psum_scatter(
        partial_recon.astype(jnp.bfloat16), "feat", scatter_dimension=1, tiled=True
    ).astype(jnp.float32)
    share = recon_share.shape[1]
    start = lax.axis_index("feat") * share
    own_x = lax.dynamic_slice_in_dim(rows_x, start, share, 1)
    own_g = lax.dynamic_slice_in_dim(rows_g, start, share, 1)
    recon = recon_share + b_dec
    error = own_x.astype(jnp.float32) - recon
    local_terms = jnp.sum(error * own_g.astype(jnp.float32), axis=1)
    error_attr = lax.psum(local_terms, "feat")
    proj = lax.dot_general(
        rows_g, w_dec, (((1,), (1,)), ((), ())), preferred_element_type=jnp.float32
    )
    feature_attr = acts.astype(jnp.float32) * proj
    return (feature_attr, error, error_attr)


def solution(mesh):
    placed = (
        P(None, ("tok", "feat")),
        P(None, ("tok", "feat")),
        P("tok", None),
        P(None, "feat"),
        P("feat"),
        P("feat", None),
        P("feat"),
    )
    return jax.shard_map(
        per_device,
        mesh=mesh,
        in_specs=placed,
        out_specs=(P("tok", "feat"), P("tok", "feat"), P("tok")),
        check_vma=False,
    )
```

profile of v0, /device:TPU:0, one launch (start us, length us, event | category | flops | bytes accessed | tf_op | source)
XLA Modules:
  0.0 284.6 jit_solution(3607693962824944712)
XLA Ops:
  7.2 0.0 all-gather.5.cloned.1.call-start
  7.2 0.7 all-gather.5.cloned.1.call-update
  7.9 0.0 all-gather.7.cloned.1.call-start
  7.9 0.7 all-gather.7.cloned.1.call-update
  8.6 40.8 %all-gather.5.cloned.1.call-done = bf16[2048,1024]{0,1:T(8,128)(2,1)} async-done(((bf16[2048,64]{0,1:T(8,128)(2,1)}), bf16[2048,1024]{0,1:T(8,128)(2,1)}) %all-gather.5.cloned.1.call-update) | async-done | bytes 4194320 | tf_op jit(solution)/shard_map/all_gather | solution.py:14
  49.5 6.4 %copy.20 = bf16[2048,1024]{1,0:T(8,128)(2,1)} copy(bf16[2048,1024]{0,1:T(8,128)(2,1)} %all-gather.5.cloned.1.call-done) | data formatting | bytes 8388608 | tf_op jit(solution)/shard_map/all_gather | solution.py:14
  55.8 6.6 %all-to-all-start = ((bf16[8,256,1024]{2,1,0:T(8,128)(2,1)}), bf16[8,256,1024]{2,1,0:T(8,128)(2,1)}, u32[]{:S(2)}, u32[]{:S(2)}) async-start(bf16[8,256,1024]{2,1,0:T(8,128)(2,1)} %bitcast.21), calls=%async_computation | async-start | bytes 8388608 | tf_op jit(solution)/shard_map/all_to_all | solution.py:21
  62.5 0.0 reduce-scatter.2.cloned.1.call-start
  62.5 0.0 copy-done.3
  62.5 0.2 compare_reduce_fusion
  62.7 0.1 copy.22
  62.8 0.2 mul.24
  63.1 0.2 copy.23
  63.4 59.7 %all-to-all-done = bf16[8,256,1024]{2,1,0:T(8,128)(2,1)} async-done(((bf16[8,256,1024]{2,1,0:T(8,128)(2,1)}), bf16[8,256,1024]{2,1,0:T(8,128)(2,1)}, u32[]{:S(2)}, u32[]{:S(2)}) %all-to-all-start) | async-done | bytes 4194336 | tf_op jit(solution)/shard_map/all_to_all | solution.py:21
  123.1 2.9 %copy.26 = bf16[8,32,8,1024]{3,2,0,1:T(8,128)(2,1)S(1)} copy(bf16[8,32,8,1024]{3,2,1,0:T(8,128)(2,1)} %bitcast.4) | data formatting | bytes 8388608 | tf_op jit(solution)/shard_map/all_to_all | solution.py:21
  126.0 0.0 copy-start
  126.0 2.0 copy-done
  127.9 0.0 copy-done.4
  127.9 6.5 %fusion.2 = bf16[256,640]{1,0:T(8,128)(2,1)S(1)} fusion(f32[256,640]{1,0:T(8,128)S(1)} %copy.23, bf16[256,8192]{1,0:T(8,128)(2,1)S(1)} %bitcast.23, bf16[8192,640]{1,0:T(8,128)(2,1)} %param.10, f32[640]{0:T(1024)S(1)} %copy-done.4), kind=kOutput, calls=%fused_computation.5 | convolution fusion | flops 2685009920 | bytes 15665664 | tf_op jit(solution)/shard_map/dot_general | solution.py:30
  134.4 4.9 %convolution_convert_fusion = bf16[256,8192]{1,0:T(8,128)(2,1)} fusion(bf16[256,640]{1,0:T(8,128)(2,1)S(1)} %fusion.2, bf16[640,8192]{1,0:T(8,128)(2,1)S(1)} %bitcast.30), kind=kOutput, calls=%fused_computation | convolution fusion | flops 2686451712 | bytes 15007744 | tf_op jit(solution)/shard_map/dot_general | solution.py:33
  139.4 0.0 reduce-scatter.2.cloned.1.call-update
  139.4 0.0 all-gather.7.cloned.1.call-done
  139.4 6.4 %copy.24 = bf16[2048,1024]{1,0:T(8,128)(2,1)} copy(bf16[2048,1024]{0,1:T(8,128)(2,1)} %all-gather.7.cloned.1.call-done) | data formatting | bytes 8388608 | tf_op jit(solution)/shard_map/all_gather | solution.py:15
  145.8 4.8 %all-to-all-start.1 = ((bf16[8,256,1024]{2,1,0:T(8,128)(2,1)}), bf16[8,256,1024]{2,1,0:T(8,128)(2,1)}, u32[]{:S(2)}, u32[]{:S(2)}) async-start(bf16[8,256,1024]{2,1,0:T(8,128)(2,1)} %bitcast.22), calls=%async_computation.1 | async-start | bytes 8388608 | tf_op jit(solution)/shard_map/all_to_all | solution.py:22
  150.6 61.9 %all-to-all-done.1 = bf16[8,256,1024]{2,1,0:T(8,128)(2,1)} async-done(((bf16[8,256,1024]{2,1,0:T(8,128)(2,1)}), bf16[8,256,1024]{2,1,0:T(8,128)(2,1)}, u32[]{:S(2)}, u32[]{:S(2)}) %all-to-all-start.1) | async-done | bytes 4194336 | tf_op jit(solution)/shard_map/all_to_all | solution.py:22
  212.5 2.7 copy.27
  215.2 0.0 copy-start.1
  215.2 1.9 copy-done.1
  217.1 7.1 %convolution_multiply_fusion = f32[256,640]{1,0:T(8,128)} fusion(bf16[256,8192]{1,0:T(8,128)(2,1)S(1)} %bitcast.25, bf16[640,8192]{1,0:T(8,128)(2,1)} %param.12, bf16[256,640]{1,0:T(8,128)(2,1)S(1)} %fusion.2), kind=kOutput, calls=%fused_computation.1 | convolution fusion | flops 2684682240 | bytes 15663104 | tf_op jit(solution)/shard_map/dot_general | solution.py:45
  224.2 22.1 %reduce-scatter.2.cloned.1.call-done = bf16[256,512]{1,0:T(8,128)(2,1)} async-done(((bf16[256,8192]{1,0:T(8,128)(2,1)}), bf16[256,512]{1,0:T(8,128)(2,1)}) %reduce-scatter.2.cloned.1.call-update) | async-done | bytes 262160 | tf_op jit(solution)/shard_map/reduce_scatter | solution.py:34
  246.3 2.0 multiply_reduce_fusion
  248.3 29.7 %psum.7 = f32[256]{0:T(256)} all-reduce(f32[256]{0:T(256)S(1)} %get-tuple-element.3), channel_id=1, replica_groups=mesh['tok'=8,'feat'=16] {'feat'}, use_global_device_ids=true, to_apply=%region_3.0 | all-reduce | flops 256 | bytes 2048 | tf_op jit(solution)/shard_map/psum | solution.py:44
  (14 shorter events, 0.1 us)
Async XLA Ops:
  7.2 42.3 %all-gather.5.cloned.1.call-start = ((), (), s32[]{:S(2)}) async-start(), calls=%async_computation.4 | async-start | bytes 4456448 | tf_op jit(solution)/shard_map/all_gather | solution.py:14
  7.9 131.5 %all-gather.7.cloned.1.call-start = ((), (), s32[]{:S(2)}) async-start(), calls=%async_computation.5 | async-start | bytes 4456448 | tf_op jit(solution)/shard_map/all_gather | solution.py:15
  55.8 6.7 %copy-start.3 = (s32[2,20]{1,0:T(2,128)S(1)}, s32[2,20]{1,0:T(2,128)}, u32[]{:S(2)}) copy-start(s32[2,20]{1,0:T(2,128)} %param.9) | copy-start | bytes 484
  55.8 67.2 %all-to-all-start = ((bf16[8,256,1024]{2,1,0:T(8,128)(2,1)}), bf16[8,256,1024]{2,1,0:T(8,128)(2,1)}, u32[]{:S(2)}, u32[]{:S(2)}) async-start(bf16[8,256,1024]{2,1,0:T(8,128)(2,1)} %bitcast.21), calls=%async_computation | async-start | bytes 8388608 | tf_op jit(solution)/shard_map/all_to_all | solution.py:21
  62.5 183.8 %reduce-scatter.2.cloned.1.call-start = ((), (), s32[]{:S(2)}) async-start(), calls=%async_computation.3 | async-start | bytes 4456448 | tf_op jit(solution)/shard_map/reduce_scatter | solution.py:34
  123.1 4.9 %copy-start.4 = (f32[640]{0:T(1024)S(1)}, f32[640]{0:T(1024)}, u32[]{:S(2)}) copy-start(f32[640]{0:T(1024)} %param.11) | copy-start | bytes 7684
  123.1 11.3 %slice-start = ((s8[10485760]{0:T(1024)(128)(4,1)}), s8[4194304]{0:T(1024)(128)(4,1)S(1)}, s32[]{:S(2)}) async-start(s8[10485760]{0:T(1024)(128)(4,1)} %bitcast.29), calls=%async_computation.6 | async-start | bytes 8388608
  126.0 2.0 copy-start
  127.9 6.5 %slice-start.1 = ((s8[10485760]{0:T(1024)(128)(4,1)}), s8[4194304]{0:T(1024)(128)(4,1)S(1)}, s32[]{:S(2)}) async-start(s8[10485760]{0:T(1024)(128)(4,1)} %bitcast.29), calls=%async_computation.7 | async-start | bytes 8388608
  127.9 6.5 %slice-start.2 = ((s8[10485760]{0:T(1024)(128)(4,1)}), s8[2097152]{0:T(1024)(128)(4,1)S(1)}, s32[]{:S(2)}) async-start(s8[10485760]{0:T(1024)(128)(4,1)} %bitcast.29), calls=%async_computation.8 | async-start | bytes 4194304
  145.8 66.7 %all-to-all-start.1 = ((bf16[8,256,1024]{2,1,0:T(8,128)(2,1)}), bf16[8,256,1024]{2,1,0:T(8,128)(2,1)}, u32[]{:S(2)}, u32[]{:S(2)}) async-start(bf16[8,256,1024]{2,1,0:T(8,128)(2,1)} %bitcast.22), calls=%async_computation.1 | async-start | bytes 8388608 | tf_op jit(solution)/shard_map/all_to_all | solution.py:22
  215.2 1.9 copy-start.1
  217.1 29.2 %copy-start.2 = (f32[512]{0:T(512)S(1)}, f32[512]{0:T(512)}, u32[]{:S(2)}) copy-start(f32[512]{0:T(512)} %param.13) | copy-start | bytes 6148
Sparse Core Ops, SparseCore 0:
  9.7 39.7 all-gather.4
  51.2 79.7 all-gather.6
  139.5 106.7 reduce-scatter.1
where the time goes:
time: 285 us
  waiting for transfers between devices  186 us (65%)
  blocking collectives  29.7 us (10%)
  local copies, waits for them, and re-layouts  22.8 us (8%)
  matrix products  18.5 us (6%)
  between operations  13.9 us (5%)
  starting transfers between devices  11.6 us (4%)
    all_to_all x1, waiting for transfers between devices, per_device(): lax.all_to_all(cols_g, 'tok', split_axis=0, concat_axis=1, tiled=True)  61.9 us
    all_to_all x1, waiting for transfers between devices, per_device(): lax.all_to_all(cols_x, 'tok', split_axis=0, concat_axis=1, tiled=True)  59.7 us
    all_gather x1, waiting for transfers between devices, per_device(): lax.all_gather(resid[:, None, :], 'feat', axis=1, tiled=True)  40.8 us
    psum x1, blocking collectives, per_device(): error_attr = lax.psum(local_terms, 'feat')  29.7 us
    reduce_scatter x1, waiting for transfers between devices, per_device(): lax.psum_scatter(partial_recon.astype(jnp.bfloat16), 'feat', scatter_dime...  22.1 us
    dot_general x1, matrix products, per_device(): lax.dot_general(rows_g, w_dec, (((1,), (1,)), ((), ())), preferred_elemen...  7.11 us
    all_to_all x1, starting transfers between devices, per_device(): lax.all_to_all(cols_x, 'tok', split_axis=0, concat_axis=1, tiled=True)  6.65 us
    dot_general x1, matrix products, per_device(): pre = jnp.dot(rows_x, w_enc, preferred_element_type=jnp.float32) + b_enc  6.46 us
  transfers between devices with their start and end apart: 5, of which 4 were waited for; matrix products, arithmetic and copies ran while one was open for 13% of the time, Pallas kernels for 0%

commit v1 on v0

--- a/solution.py
+++ b/solution.py
@@ -41,7 +41,7 @@
     recon = recon_share + b_dec
     error = own_x.astype(jnp.float32) - recon
     local_terms = jnp.sum(error * own_g.astype(jnp.float32), axis=1)
-    error_attr = lax.psum(local_terms, "feat")
+    error_attr = jnp.sum(lax.all_gather(local_terms, axis_name="feat"), 0)
     proj = lax.dot_general(
         rows_g, w_dec, (((1,), (1,)), ((), ())), preferred_element_type=jnp.float32
     )

time: 285 us -> 273 us (0.958)
  blocking collectives: 29.7 us -> 16 us
    psum x1 -> x0, blocking collectives: 29.7 us -> none  [per_device(): error_attr = lax.psum(local_terms, 'feat')]
    all_gather x0 -> x1, blocking collectives: none -> 16 us  [per_device(): error_attr = jnp.sum(lax.all_gather(local_terms, axis_name='feat'), 0)]
  transfers between devices with their start and end apart: 5 -> 5, of which waited for: 4 -> 4; matrix products, arithmetic and copies ran while one was open for 13% -> 14% of each run, Pallas kernels for 0% -> 0%
where the time goes in v1:
time: 273 us; the launch traced here: 272 us
  waiting for transfers between devices  186 us (68%)
  local copies, waits for them, and re-layouts  22.8 us (8%)
  matrix products  18.6 us (7%)
  blocking collectives  16 us (6%)
  between operations  13.9 us (5%)
  starting transfers between devices  11.6 us (4%)
  other arithmetic  2.81 us (1%)
    all_to_all x1, waiting for transfers between devices, per_device(): lax.all_to_all(cols_g, 'tok', split_axis=0, concat_axis=1, tiled=True)  61.6 us
    all_to_all x1, waiting for transfers between devices, per_device(): lax.all_to_all(cols_x, 'tok', split_axis=0, concat_axis=1, tiled=True)  59.7 us
    all_gather x1, waiting for transfers between devices, per_device(): lax.all_gather(resid[:, None, :], 'feat', axis=1, tiled=True)  40.8 us
    reduce_scatter x1, waiting for transfers between devices, per_device(): lax.psum_scatter(partial_recon.astype(jnp.bfloat16), 'feat', scatter_dime...  22.5 us
    all_gather x1, blocking collectives, per_device(): error_attr = jnp.sum(lax.all_gather(local_terms, axis_name='feat'), 0)  16 us
    dot_general x1, matrix products, per_device(): lax.dot_general(rows_g, w_dec, (((1,), (1,)), ((), ())), preferred_elemen...  7.11 us
    all_to_all x1, starting transfers between devices, per_device(): lax.all_to_all(cols_x, 'tok', split_axis=0, concat_axis=1, tiled=True)  6.65 us
    dot_general x1, matrix products, per_device(): pre = jnp.dot(rows_x, w_enc, preferred_element_type=jnp.float32) + b_enc  6.46 us
  transfers between devices with their start and end apart: 5, of which 4 were waited for; matrix products, arithmetic and copies ran while one was open for 14% of the time, Pallas kernels for 0%

profile of v1, /device:TPU:0, one launch (start us, length us, event | category | flops | bytes accessed | tf_op | source)
XLA Modules:
  0.0 271.6 jit_solution(2767278541426732856)
XLA Ops:
  7.2 0.0 all-gather.7.cloned.1.call-start
  7.2 0.7 all-gather.7.cloned.1.call-update
  7.9 0.0 all-gather.9.cloned.1.call-start
  7.9 0.7 all-gather.9.cloned.1.call-update
  8.6 40.8 %all-gather.7.cloned.1.call-done = bf16[2048,1024]{0,1:T(8,128)(2,1)} async-done(((bf16[2048,64]{0,1:T(8,128)(2,1)}), bf16[2048,1024]{0,1:T(8,128)(2,1)}) %all-gather.7.cloned.1.call-update) | async-done | bytes 4194320 | tf_op jit(solution)/shard_map/all_gather | solution.py:14
  49.5 6.4 %copy.20 = bf16[2048,1024]{1,0:T(8,128)(2,1)} copy(bf16[2048,1024]{0,1:T(8,128)(2,1)} %all-gather.7.cloned.1.call-done) | data formatting | bytes 8388608 | tf_op jit(solution)/shard_map/all_gather | solution.py:14
  55.8 6.6 %all-to-all-start = ((bf16[8,256,1024]{2,1,0:T(8,128)(2,1)}), bf16[8,256,1024]{2,1,0:T(8,128)(2,1)}, u32[]{:S(2)}, u32[]{:S(2)}) async-start(bf16[8,256,1024]{2,1,0:T(8,128)(2,1)} %bitcast.22), calls=%async_computation | async-start | bytes 8388608 | tf_op jit(solution)/shard_map/all_to_all | solution.py:21
  62.5 0.0 reduce-scatter.2.cloned.1.call-start
  62.5 0.0 copy-done.3
  62.5 0.2 compare_reduce_fusion
  62.7 0.1 copy.22
  62.8 0.2 mul.24
  63.1 0.2 copy.23
  63.4 59.7 %all-to-all-done = bf16[8,256,1024]{2,1,0:T(8,128)(2,1)} async-done(((bf16[8,256,1024]{2,1,0:T(8,128)(2,1)}), bf16[8,256,1024]{2,1,0:T(8,128)(2,1)}, u32[]{:S(2)}, u32[]{:S(2)}) %all-to-all-start) | async-done | bytes 4194336 | tf_op jit(solution)/shard_map/all_to_all | solution.py:21
  123.1 2.9 %copy.26 = bf16[8,32,8,1024]{3,2,0,1:T(8,128)(2,1)S(1)} copy(bf16[8,32,8,1024]{3,2,1,0:T(8,128)(2,1)} %bitcast.5) | data formatting | bytes 8388608 | tf_op jit(solution)/shard_map/all_to_all | solution.py:21
  126.0 0.0 copy-start
  126.0 2.0 copy-done
  127.9 0.0 copy-done.4
  127.9 6.5 %fusion.2 = bf16[256,640]{1,0:T(8,128)(2,1)S(1)} fusion(f32[256,640]{1,0:T(8,128)S(1)} %copy.23, bf16[256,8192]{1,0:T(8,128)(2,1)S(1)} %bitcast.24, bf16[8192,640]{1,0:T(8,128)(2,1)} %param.10, f32[640]{0:T(1024)S(1)} %copy-done.4), kind=kOutput, calls=%fused_computation.5 | convolution fusion | flops 2685009920 | bytes 15665664 | tf_op jit(solution)/shard_map/dot_general | solution.py:30
  134.4 5.0 %convolution_convert_fusion = bf16[256,8192]{1,0:T(8,128)(2,1)} fusion(bf16[256,640]{1,0:T(8,128)(2,1)S(1)} %fusion.2, bf16[640,8192]{1,0:T(8,128)(2,1)S(1)} %bitcast.32), kind=kOutput, calls=%fused_computation | convolution fusion | flops 2686451712 | bytes 15007744 | tf_op jit(solution)/shard_map/dot_general | solution.py:33
  139.5 0.0 reduce-scatter.2.cloned.1.call-update
  139.5 0.0 all-gather.9.cloned.1.call-done
  139.5 6.4 %copy.24 = bf16[2048,1024]{1,0:T(8,128)(2,1)} copy(bf16[2048,1024]{0,1:T(8,128)(2,1)} %all-gather.9.cloned.1.call-done) | data formatting | bytes 8388608 | tf_op jit(solution)/shard_map/all_gather | solution.py:15
  145.9 4.8 %all-to-all-start.1 = ((bf16[8,256,1024]{2,1,0:T(8,128)(2,1)}), bf16[8,256,1024]{2,1,0:T(8,128)(2,1)}, u32[]{:S(2)}, u32[]{:S(2)}) async-start(bf16[8,256,1024]{2,1,0:T(8,128)(2,1)} %bitcast.23), calls=%async_computation.1 | async-start | bytes 8388608 | tf_op jit(solution)/shard_map/all_to_all | solution.py:22
  150.7 61.6 %all-to-all-done.1 = bf16[8,256,1024]{2,1,0:T(8,128)(2,1)} async-done(((bf16[8,256,1024]{2,1,0:T(8,128)(2,1)}), bf16[8,256,1024]{2,1,0:T(8,128)(2,1)}, u32[]{:S(2)}, u32[]{:S(2)}) %all-to-all-start.1) | async-done | bytes 4194336 | tf_op jit(solution)/shard_map/all_to_all | solution.py:22
  212.3 2.7 copy.27
  215.0 1.9 copy-done.1
  216.9 7.1 %convolution_multiply_fusion = f32[256,640]{1,0:T(8,128)} fusion(bf16[256,8192]{1,0:T(8,128)(2,1)S(1)} %bitcast.26, bf16[640,8192]{1,0:T(8,128)(2,1)} %param.12, bf16[256,640]{1,0:T(8,128)(2,1)S(1)} %fusion.2), kind=kOutput, calls=%fused_computation.1 | convolution fusion | flops 2684682240 | bytes 15663104 | tf_op jit(solution)/shard_map/dot_general | solution.py:45
  224.0 22.5 %reduce-scatter.2.cloned.1.call-done = bf16[256,512]{1,0:T(8,128)(2,1)} async-done(((bf16[256,8192]{1,0:T(8,128)(2,1)}), bf16[256,512]{1,0:T(8,128)(2,1)}) %reduce-scatter.2.cloned.1.call-update) | async-done | bytes 262160 | tf_op jit(solution)/shard_map/reduce_scatter | solution.py:34
  246.5 2.0 multiply_reduce_fusion
  248.5 16.0 %all-gather.3 = f32[16,1,256]{2,1,0:T(1,128)S(1)} all-gather(f32[1,1,256]{2,1,0:T(1,128)S(1)} %bitcast.30), channel_id=4, replica_groups=mesh['tok'=8,'feat'=16] {'feat'}, dimensions={0}, use_global_device_ids=true | all-gather | bytes 17408 | tf_op jit(solution)/shard_map/all_gather | solution.py:44
  264.5 0.6 reduce_sum.19
  (15 shorter events, 0.1 us)
Async XLA Ops:
  7.2 42.3 %all-gather.7.cloned.1.call-start = ((), (), s32[]{:S(2)}) async-start(), calls=%async_computation.4 | async-start | bytes 4456448 | tf_op jit(solution)/shard_map/all_gather | solution.py:14
  7.9 131.6 %all-gather.9.cloned.1.call-start = ((), (), s32[]{:S(2)}) async-start(), calls=%async_computation.5 | async-start | bytes 4456448 | tf_op jit(solution)/shard_map/all_gather | solution.py:15
  55.8 6.7 %copy-start.3 = (s32[2,20]{1,0:T(2,128)S(1)}, s32[2,20]{1,0:T(2,128)}, u32[]{:S(2)}) copy-start(s32[2,20]{1,0:T(2,128)} %param.9) | copy-start | bytes 484
  55.8 67.2 %all-to-all-start = ((bf16[8,256,1024]{2,1,0:T(8,128)(2,1)}), bf16[8,256,1024]{2,1,0:T(8,128)(2,1)}, u32[]{:S(2)}, u32[]{:S(2)}) async-start(bf16[8,256,1024]{2,1,0:T(8,128)(2,1)} %bitcast.22), calls=%async_computation | async-start | bytes 8388608 | tf_op jit(solution)/shard_map/all_to_all | solution.py:21
  62.5 184.0 %reduce-scatter.2.cloned.1.call-start = ((), (), s32[]{:S(2)}) async-start(), calls=%async_computation.3 | async-start | bytes 4456448 | tf_op jit(solution)/shard_map/reduce_scatter | solution.py:34
  123.1 4.9 %copy-start.4 = (f32[640]{0:T(1024)S(1)}, f32[640]{0:T(1024)}, u32[]{:S(2)}) copy-start(f32[640]{0:T(1024)} %param.11) | copy-start | bytes 7684
  123.1 11.3 %slice-start = ((s8[10485760]{0:T(1024)(128)(4,1)}), s8[4194304]{0:T(1024)(128)(4,1)S(1)}, s32[]{:S(2)}) async-start(s8[10485760]{0:T(1024)(128)(4,1)} %bitcast.31), calls=%async_computation.6 | async-start | bytes 8388608
  126.0 2.0 copy-start
  127.9 6.5 %slice-start.1 = ((s8[10485760]{0:T(1024)(128)(4,1)}), s8[4194304]{0:T(1024)(128)(4,1)S(1)}, s32[]{:S(2)}) async-start(s8[10485760]{0:T(1024)(128)(4,1)} %bitcast.31), calls=%async_computation.7 | async-start | bytes 8388608
  127.9 6.5 %slice-start.2 = ((s8[10485760]{0:T(1024)(128)(4,1)}), s8[2097152]{0:T(1024)(128)(4,1)S(1)}, s32[]{:S(2)}) async-start(s8[10485760]{0:T(1024)(128)(4,1)} %bitcast.31), calls=%async_computation.8 | async-start | bytes 4194304
  145.9 66.4 %all-to-all-start.1 = ((bf16[8,256,1024]{2,1,0:T(8,128)(2,1)}), bf16[8,256,1024]{2,1,0:T(8,128)(2,1)}, u32[]{:S(2)}, u32[]{:S(2)}) async-start(bf16[8,256,1024]{2,1,0:T(8,128)(2,1)} %bitcast.23), calls=%async_computation.1 | async-start | bytes 8388608 | tf_op jit(solution)/shard_map/all_to_all | solution.py:22
  215.0 1.9 copy-start.1
  216.9 29.6 %copy-start.2 = (f32[512]{0:T(512)S(1)}, f32[512]{0:T(512)}, u32[]{:S(2)}) copy-start(f32[512]{0:T(512)} %param.13) | copy-start | bytes 6148
Sparse Core Ops, SparseCore 0:
  9.7 39.7 all-gather.6
  51.2 79.7 all-gather.8
  139.6 106.8 reduce-scatter.1
